TPU v7x, 32 devices: a whole 2x2x4 slice. The times are simulated.
32 devices in a mesh: groups: 2 (over x), width: 16 (over z, y, core).
Axes of the slice: x: 2, y: 2, z: 4, core: 2. Of those that a mesh axis runs over, the one named last changes fastest.
Arguments:
- stream_in: bfloat16 [2, 128, 8192], P(None, 'groups', 'width'), parts along dimension 1, may hold values from -16 to 16
- norm_gain: float32 [2, 8192], replicated, may hold values from 0.1 to 1.9
- w_gate: bfloat16 [2, 8192, 14336], P(None, None, 'width'), may hold values from -0.0625 to 0.0625
- w_up: bfloat16 [2, 8192, 14336], P(None, None, 'width'), may hold values from -0.0625 to 0.0625
- w_down: bfloat16 [2, 14336, 8192], P(None, 'width'), may hold values from -0.0625 to 0.0625
Outputs:
- stream_out: bfloat16 [2, 128, 8192], P(None, 'groups', 'width'), parts along dimension 1
There are 2 independent parts, one for each index of `groups`. A program takes and returns all parts, laid end to end along the dimension named above; an argument that names none is the same for every part. Nothing has to cross between parts.
All inputs are finite; a program needn't handle non-finite values.
Results may differ from a plain program's by a relative error of at most 0.012.
Values may be sent and summed in bfloat16 or wider, within the bound.
A program may use at most 192 MiB of HBM per device.

v0:
```python
import jax
import jax.numpy as jnp
from jax import lax
from jax.sharding import PartitionSpec as P

LAYERS = 2
MICRO = 2


def body(stream_in, norm_gain, w_gate, w_up, w_down):
    width_local = stream_in.shape[2]
    offset = lax.axis_index("width") * width_local
    starts = [
        lax.all_gather(stream_in[micro_index], "width", axis=1, tiled=True)
        for micro_index in range(MICRO)
    ]
    results = []
    for micro_index in range(MICRO):
        stream = starts[micro_index]
        for depth in range(LAYERS):
            stream_f = stream.astype(jnp.float32)
            meansq = jnp.mean(stream_f * stream_f, axis=1, keepdims=True)
            normed = (stream_f * lax.rsqrt(meansq + 1e-05) * norm_gain[depth]).astype(jnp.bfloat16)
            gate_out = jnp.dot(normed, w_gate[depth], preferred_element_type=jnp.float32)
            up_out = jnp.dot(normed, w_up[depth], preferred_element_type=jnp.float32)
            hidden = (jax.nn.silu(gate_out) * up_out).astype(jnp.bfloat16)
            partials = jnp.dot(hidden, w_down[depth], preferred_element_type=jnp.float32)
            branch = lax.psum(partials, "width")
            stream = (stream_f + branch).astype(jnp.bfloat16)
        results.append(stream)
    results = [lax.dynamic_slice_in_dim(stream, offset, width_local, 1) for stream in results]
    return jnp.stack(results)


def solution(mesh):
    return jax.shard_map(
        body,
        mesh=mesh,
        in_specs=(
            P(None, "groups", "width"),
            P(),
            P(None, None, "width"),
            P(None, None, "width"),
            P(None, "width", None),
        ),
        out_specs=P(None, "groups", "width"),
        check_vma=False,
    )
```

profile of v0, /device:TPU:0, one launch (start us, length us, event | category | flops | bytes accessed | tf_op | source)
XLA Modules:
  0.0 415.5 jit_solution(16510495588360910265)
XLA Ops:
  6.5 0.0 all-gather.5.cloned.1.call-start
  6.5 1.5 fusion.118
  8.1 0.0 all-gather.5.cloned.1.call-update
  8.1 0.0 all-gather.7.cloned.1.call-start
  8.1 0.7 all-gather.7.cloned.1.call-update
  8.8 0.0 all-reduce.7.cloned.1.call-start
  8.9 1.0 fusion.119
  9.9 39.0 %all-gather.5.cloned.1.call-done = bf16[1,64,8192]{2,1,0:T(8,128)(2,1)} async-done(((bf16[1,64,512]{2,1,0:T(8,128)(2,1)}), bf16[1,64,8192]{2,1,0:T(8,128)(2,1)}) %all-gather.5.cloned.1.call-update) | async-done | bytes 1048592 | tf_op jit(solution)/shard_map/all_gather | solution.py:14
  48.9 1.6 fusion.36
  50.5 36.8 %all-gather.7.cloned.1.call-done = bf16[1,64,8192]{2,1,0:T(8,128)(2,1)} async-done(((bf16[1,64,512]{2,1,0:T(8,128)(2,1)}), bf16[1,64,8192]{2,1,0:T(8,128)(2,1)}) %all-gather.7.cloned.1.call-update) | async-done | bytes 1048592 | tf_op jit(solution)/shard_map/all_gather | solution.py:14
  87.3 1.5 fusion.40
  88.9 0.0 copy-done
  88.9 0.0 copy-start.1
  88.9 6.7 %fusion.22 = f32[64,896]{1,0:T(8,128)S(1)} fusion(bf16[2,8192,896]{2,1,0:T(8,128)(2,1)} %param.7, bf16[1,64,8192]{2,1,0:T(8,128)(2,1)S(1)} %copy-done, f32[8192]{0:T(1024)S(1)} %bitcast.82, f32[64]{0:T(128)S(1)} %add_rsqrt_fusion.3), kind=kOutput, calls=%fused_computation.22 | convolution fusion | flops 941621248 | bytes 15991040 | tf_op jit(solution)/shard_map/dot_general | solution.py:24
  95.6 6.6 %fusion.20 = f32[64,896]{1,0:T(8,128)S(1)} fusion(bf16[2,8192,896]{2,1,0:T(8,128)(2,1)} %param.7, bf16[1,64,8192]{2,1,0:T(8,128)(2,1)S(1)} %copy-done.1, f32[64]{0:T(128)S(1)} %add_rsqrt_fusion.1, f32[8192]{0:T(1024)S(1)} %bitcast.83), kind=kOutput, calls=%fused_computation.20 | convolution fusion | flops 941621248 | bytes 15991040 | tf_op jit(solution)/shard_map/dot_general | solution.py:24
  102.2 16.4 %fusion.14 = f32[64,8192]{1,0:T(8,128)} fusion(bf16[2,896,8192]{2,1,0:T(8,128)(2,1)} %param.9, bf16[2,8192,896]{2,1,0:T(8,128)(2,1)} %param.8, bf16[1,64,8192]{2,1,0:T(8,128)(2,1)S(1)} %copy-done, f32[8192]{0:T(1024)S(1)} %bitcast.84, f32[64]{0:T(128)S(1)} %add_rsqrt_fusion.3, f32[64,896]{1,0:T(8,128)S(1)} %fusion.22), kind=kOutput, calls=%fused_computation.14 | convolution fusion | flops 1881489408 | bytes 32768256 | tf_op jit(solution)/shard_map/dot_general | solution.py:27
  118.6 16.3 %fusion.12 = f32[64,8192]{1,0:T(8,128)} fusion(bf16[2,896,8192]{2,1,0:T(8,128)(2,1)} %param.9, bf16[2,8192,896]{2,1,0:T(8,128)(2,1)} %param.8, bf16[1,64,8192]{2,1,0:T(8,128)(2,1)S(1)} %copy-done.1, f32[64]{0:T(128)S(1)} %add_rsqrt_fusion.1, f32[8192]{0:T(1024)S(1)} %bitcast.85, f32[64,896]{1,0:T(8,128)S(1)} %fusion.20), kind=kOutput, calls=%fused_computation.12 | convolution fusion | flops 1881489408 | bytes 32768256 | tf_op jit(solution)/shard_map/dot_general | solution.py:27
  134.9 0.0 all-reduce.7.cloned.1.call-update
  134.9 0.2 all-reduce.5.cloned.1.call-start
  135.2 110.9 %all-reduce.7.cloned.1.call-done = (f32[64,8192]{1,0:T(8,128)}, f32[64,8192]{1,0:T(8,128)}) async-done(((f32[64,8192]{1,0:T(8,128)}, f32[64,8192]{1,0:T(8,128)}), (f32[64,8192]{1,0:T(8,128)}, f32[64,8192]{1,0:T(8,128)})) %all-reduce.7.cloned.1.call-update) | async-done | bytes 4194320 | tf_op jit(solution)/shard_map/psum | solution.py:28
  246.0 4.2 %multiply_reduce_fusion = (f32[64]{0:T(128)S(1)}, f32[64,8192]{1,0:T(8,128)}, f32[64]{0:T(128)S(1)}, f32[64,8192]{1,0:T(8,128)S(1)}) fusion(f32[64,8192]{1,0:T(8,128)} %get-tuple-element.7, bf16[1,64,8192]{2,1,0:T(8,128)(2,1)S(1)} %copy-done.1, f32[64,8192]{1,0:T(8,128)} %get-tuple-element.8, bf16[1,64,8192]{2,1,0:T(8,128)(2,1)S(1)} %copy-done), kind=kLoop, calls=%fused_computation.51 | loop fusion | flops 6291328 | bytes 10486272 | tf_op jit(solution)/shard_map/reduce_sum | solution.py:22
  250.2 1.3 copy-done.3
  251.6 6.6 %fusion.10 = f32[64,896]{1,0:T(8,128)S(1)} fusion(bf16[2,8192,896]{2,1,0:T(8,128)(2,1)} %param.7, f32[64,8192]{1,0:T(8,128)S(1)} %get-tuple-element.18, f32[8192]{0:T(1024)S(1)} %bitcast.78, f32[64]{0:T(128)S(1)} %add_rsqrt_fusion.2), kind=kOutput, calls=%fused_computation.10 | convolution fusion | flops 941096960 | bytes 17039616 | tf_op jit(solution)/shard_map/dot_general | solution.py:24
  258.2 14.6 %fusion.2 = f32[64,8192]{1,0:T(8,128)} fusion(bf16[2,896,8192]{2,1,0:T(8,128)(2,1)} %param.9, bf16[2,8192,896]{2,1,0:T(8,128)(2,1)} %param.8, f32[64,896]{1,0:T(8,128)S(1)} %fusion.10, f32[64,8192]{1,0:T(8,128)} %copy-done.3, f32[8192]{0:T(1024)S(1)} %bitcast.79, f32[64]{0:T(128)S(1)} %add_rsqrt_fusion.2), kind=kOutput, calls=%fused_computation.2 | convolution fusion | flops 1880965120 | bytes 33816832 | tf_op jit(solution)/shard_map/dot_general | solution.py:27
  272.8 0.0 copy-done.2
  272.8 6.6 %fusion.8 = f32[64,896]{1,0:T(8,128)S(1)} fusion(bf16[2,8192,896]{2,1,0:T(8,128)(2,1)} %param.7, f32[64,8192]{1,0:T(8,128)S(1)} %copy-done.2, f32[64]{0:T(128)S(1)} %add_rsqrt_fusion, f32[8192]{0:T(1024)S(1)} %bitcast.80), kind=kOutput, calls=%fused_computation.8 | convolution fusion | flops 941096960 | bytes 17039616 | tf_op jit(solution)/shard_map/dot_general | solution.py:24
  279.5 16.4 %fusion = f32[64,8192]{1,0:T(8,128)} fusion(bf16[2,896,8192]{2,1,0:T(8,128)(2,1)} %param.9, bf16[2,8192,896]{2,1,0:T(8,128)(2,1)} %param.8, f32[64,896]{1,0:T(8,128)S(1)} %fusion.8, f32[64,8192]{1,0:T(8,128)S(1)} %copy-done.2, f32[64]{0:T(128)S(1)} %add_rsqrt_fusion, f32[8192]{0:T(1024)S(1)} %bitcast.81), kind=kOutput, calls=%fused_computation | convolution fusion | flops 1880965120 | bytes 33816832 | tf_op jit(solution)/shard_map/dot_general | solution.py:27
  295.8 0.0 all-reduce.5.cloned.1.call-update
  295.9 110.6 %all-reduce.5.cloned.1.call-done = (f32[64,8192]{1,0:T(8,128)}, f32[64,8192]{1,0:T(8,128)}) async-done(((f32[64,8192]{1,0:T(8,128)}, f32[64,8192]{1,0:T(8,128)}), (f32[64,8192]{1,0:T(8,128)}, f32[64,8192]{1,0:T(8,128)})) %all-reduce.5.cloned.1.call-update) | async-done | bytes 4194320 | tf_op jit(solution)/shard_map/psum | solution.py:28
  406.4 1.0 fusion.110
  407.4 0.9 fusion.111
  408.3 0.7 pad_maximum_fusion
  (8 shorter events, 0.0 us)
Async XLA Ops:
  6.5 42.4 %all-gather.5.cloned.1.call-start = ((), (), s32[]{:S(2)}) async-start(), calls=%async_computation | async-start | bytes 1114112 | tf_op jit(solution)/shard_map/all_gather | solution.py:14
  8.1 79.3 %all-gather.7.cloned.1.call-start = ((), (), s32[]{:S(2)}) async-start(), calls=%async_computation.1 | async-start | bytes 1114112 | tf_op jit(solution)/shard_map/all_gather | solution.py:14
  8.8 237.2 %all-reduce.7.cloned.1.call-start = ((), (), s32[]{:S(2)}) async-start(), calls=%async_computation.3 | async-start | bytes 8388608 | tf_op jit(solution)/shard_map/psum | solution.py:28
  48.9 40.0 %copy-start = (bf16[1,64,8192]{2,1,0:T(8,128)(2,1)S(1)}, bf16[1,64,8192]{2,1,0:T(8,128)(2,1)}, u32[]{:S(2)}) copy-start(bf16[1,64,8192]{2,1,0:T(8,128)(2,1)} %all-gather.5.cloned.1.call-done) | copy-start | bytes 3145732
  88.9 6.7 %copy-start.1 = (bf16[1,64,8192]{2,1,0:T(8,128)(2,1)S(1)}, bf16[1,64,8192]{2,1,0:T(8,128)(2,1)}, u32[]{:S(2)}) copy-start(bf16[1,64,8192]{2,1,0:T(8,128)(2,1)} %all-gather.7.cloned.1.call-done) | copy-start | bytes 3145732
  134.9 271.5 %all-reduce.5.cloned.1.call-start = ((), (), s32[]{:S(2)}) async-start(), calls=%async_computation.2 | async-start | bytes 8388608 | tf_op jit(solution)/shard_map/psum | solution.py:28
  250.2 1.4 copy-start.3
  258.2 14.6 %copy-start.2 = (f32[64,8192]{1,0:T(8,128)S(1)}, f32[64,8192]{1,0:T(8,128)}, u32[]{:S(2)}) copy-start(f32[64,8192]{1,0:T(8,128)} %get-tuple-element.12) | copy-start | bytes 6291460
Sparse Core Ops, SparseCore 0:
  9.5 39.3 all-gather.4
  51.0 36.2 all-gather.6
  135.1 110.9 all-reduce.6
  296.0 110.3 all-reduce.4
where the time goes:
time: 416 us
  waiting for transfers between devices  298 us (72%)
  matrix products  90.2 us (22%)
  between operations  13.2 us (3%)
  other arithmetic  9.94 us (2%)
    psum x2, waiting for transfers between devices, body(): branch = lax.psum(partials, 'width')  221 us
    all_gather x2, waiting for transfers between devices, body(): lax.all_gather(stream_in[micro_index], 'width', axis=1, tiled=True)  75.8 us
    dot_general x4, matrix products, body(): jnp.dot(hidden, w_down[depth], preferred_element_type=jnp.float32)  63.7 us
    dot_general x4, matrix products, body(): jnp.dot(normed, w_gate[depth], preferred_element_type=jnp.float32)  26.5 us
  transfers between devices with their start and end apart: 4, of which 4 were waited for; matrix products, arithmetic and copies ran while one was open for 1% of the time, Pallas kernels for 0%

commit v1 on v0

--- a/solution.py
+++ b/solution.py
@@ -25,7 +25,7 @@
             up_out = jnp.dot(normed, w_up[depth], preferred_element_type=jnp.float32)
             hidden = (jax.nn.silu(gate_out) * up_out).astype(jnp.bfloat16)
             partials = jnp.dot(hidden, w_down[depth], preferred_element_type=jnp.float32)
-            branch = lax.psum(partials, "width")
+            branch = jnp.sum(lax.all_gather(partials, "width"), axis=0)
             stream = (stream_f + branch).astype(jnp.bfloat16)
         results.append(stream)
     results = [lax.dynamic_slice_in_dim(stream, offset, width_local, 1) for stream in results]

time: 416 us -> 788 us (1.89)
  waiting for transfers between devices: 298 us -> 616 us
  other arithmetic: 9.94 us -> 58.7 us
    all_gather x0 -> x4, waiting for transfers between devices: none -> 564 us  [body(): branch = jnp.sum(lax.all_gather(partials, 'width'), axis=0)]
    psum x2 -> x0, waiting for transfers between devices: 221 us -> none  [body(): branch = lax.psum(partials, 'width')]
    reduce_sum x0 -> x4, other arithmetic: none -> 51.1 us  [body(): branch = jnp.sum(lax.all_gather(partials, 'width'), axis=0)]
    all_gather x2, waiting for transfers between devices: 75.8 us -> 51.1 us  [body(): lax.all_gather(stream_in[micro_index], 'width', axis=1, tiled=True)]
  transfers between devices with their start and end apart: 4 -> 6, of which waited for: 4 -> 6; matrix products, arithmetic and copies ran while one was open for 1% -> 17% of each run, Pallas kernels for 0% -> 0%
where the time goes in v1:
time: 788 us
  waiting for transfers between devices  616 us (78%)
  matrix products  93.4 us (12%)
  other arithmetic  58.7 us (7%)
  between operations  13.6 us (2%)
    all_gather x4, waiting for transfers between devices, body(): branch = jnp.sum(lax.all_gather(partials, 'width'), axis=0)  564 us
    dot_general x4, matrix products, body(): jnp.dot(hidden, w_down[depth], preferred_element_type=jnp.float32)  63.1 us
    reduce_sum x4, other arithmetic, body(): branch = jnp.sum(lax.all_gather(partials, 'width'), axis=0)  51.1 us
    all_gather x2, waiting for transfers between devices, body(): lax.all_gather(stream_in[micro_index], 'width', axis=1, tiled=True)  51.1 us
    dot_general x4, matrix products, body(): jnp.dot(normed, w_gate[depth], preferred_element_type=jnp.float32)  30.3 us
  transfers between devices with their start and end apart: 6, of which 6 were waited for; matrix products, arithmetic and copies ran while one was open for 17% of the time, Pallas kernels for 0%

profile of v1, /device:TPU:0, one launch (start us, length us, event | category | flops | bytes accessed | tf_op | source)
XLA Modules:
  0.0 787.6 jit_solution(9456301840764179438)
XLA Ops:
  6.5 1.5 fusion.118
  8.1 0.7 all-gather.19.cloned.1.call-update
  8.9 1.0 fusion.119
  9.9 39.0 %all-gather.13.cloned.1.call-done = bf16[1,64,8192]{2,1,0:T(8,128)(2,1)} async-done(((bf16[1,64,512]{2,1,0:T(8,128)(2,1)}), bf16[1,64,8192]{2,1,0:T(8,128)(2,1)}) %all-gather.13.cloned.1.call-update) | async-done | bytes 1048592 | tf_op jit(solution)/shard_map/all_gather | solution.py:14
  48.9 1.5 fusion.36
  50.4 8.2 %fusion.22 = f32[64,896]{1,0:T(8,128)S(1)} fusion(bf16[2,8192,896]{2,1,0:T(8,128)(2,1)} %param.7, bf16[1,64,8192]{2,1,0:T(8,128)(2,1)} %all-gather.13.cloned.1.call-done, f32[8192]{0:T(1024)S(1)} %bitcast.90, f32[64]{0:T(128)S(1)} %add_rsqrt_fusion.3), kind=kOutput, calls=%fused_computation.22 | convolution fusion | flops 941621248 | bytes 15991040 | tf_op jit(solution)/shard_map/dot_general | solution.py:24
  58.7 16.3 %fusion.14 = f32[64,8192]{1,0:T(8,128)} fusion(bf16[2,896,8192]{2,1,0:T(8,128)(2,1)} %param.9, bf16[2,8192,896]{2,1,0:T(8,128)(2,1)} %param.8, bf16[1,64,8192]{2,1,0:T(8,128)(2,1)S(1)} %copy-done.1, f32[8192]{0:T(1024)S(1)} %bitcast.91, f32[64]{0:T(128)S(1)} %add_rsqrt_fusion.3, f32[64,896]{1,0:T(8,128)S(1)} %fusion.22), kind=kOutput, calls=%fused_computation.14 | convolution fusion | flops 1881489408 | bytes 32768256 | tf_op jit(solution)/shard_map/dot_general | solution.py:27
  75.0 0.2 all-gather.21.cloned.1.call-start
  75.3 12.1 %all-gather.19.cloned.1.call-done = bf16[1,64,8192]{2,1,0:T(8,128)(2,1)} async-done(((bf16[1,64,512]{2,1,0:T(8,128)(2,1)}), bf16[1,64,8192]{2,1,0:T(8,128)(2,1)}) %all-gather.19.cloned.1.call-update) | async-done | bytes 1048592 | tf_op jit(solution)/shard_map/all_gather | solution.py:14
  87.3 1.5 fusion.40
  88.9 8.2 %fusion.20 = f32[64,896]{1,0:T(8,128)S(1)} fusion(bf16[2,8192,896]{2,1,0:T(8,128)(2,1)} %param.7, bf16[1,64,8192]{2,1,0:T(8,128)(2,1)} %all-gather.19.cloned.1.call-done, f32[64]{0:T(128)S(1)} %add_rsqrt_fusion.1, f32[8192]{0:T(1024)S(1)} %bitcast.92), kind=kOutput, calls=%fused_computation.20 | convolution fusion | flops 941621248 | bytes 15991040 | tf_op jit(solution)/shard_map/dot_general | solution.py:24
  97.1 16.7 %fusion.12 = f32[64,8192]{1,0:T(8,128)} fusion(bf16[2,896,8192]{2,1,0:T(8,128)(2,1)} %param.9, bf16[2,8192,896]{2,1,0:T(8,128)(2,1)} %param.8, bf16[1,64,8192]{2,1,0:T(8,128)(2,1)S(1)} %copy-done, f32[64]{0:T(128)S(1)} %add_rsqrt_fusion.1, f32[8192]{0:T(1024)S(1)} %bitcast.93, f32[64,896]{1,0:T(8,128)S(1)} %fusion.20), kind=kOutput, calls=%fused_computation.12 | convolution fusion | flops 1881489408 | bytes 32768256 | tf_op jit(solution)/shard_map/dot_general | solution.py:27
  113.8 142.8 %all-gather.15.cloned.1.call-done = f32[1024,8192]{1,0:T(8,128)} async-done(((f32[64,8192]{1,0:T(8,128)}), f32[1024,8192]{1,0:T(8,128)}) %all-gather.15.cloned.1.call-update) | async-done | bytes 33554448 | tf_op jit(solution)/shard_map/all_gather | solution.py:28
  256.6 12.7 %reduce_sum.73 = f32[64,8192]{1,0:T(8,128)S(1)} reduce(f32[16,64,8192]{2,1,0:T(8,128)} %bitcast.84, f32[]{:T(128)} %constant.18.clone.1), dimensions={0}, to_apply=%region_1.2 | reduce | flops 7864320 | bytes 35651588 | tf_op jit(solution)/shard_map/reduce_sum | solution.py:28
  269.3 1.6 multiply_reduce_fusion.1
  270.9 1.3 copy-done.2
  272.2 7.0 fusion.10
  279.2 15.0 %fusion.2 = f32[64,8192]{1,0:T(8,128)} fusion(bf16[2,896,8192]{2,1,0:T(8,128)(2,1)} %param.9, bf16[2,8192,896]{2,1,0:T(8,128)(2,1)} %param.8, f32[64,896]{1,0:T(8,128)S(1)} %fusion.10, f32[64,8192]{1,0:T(8,128)} %copy-done.2, f32[8192]{0:T(1024)S(1)} %bitcast.87, f32[64]{0:T(128)S(1)} %add_rsqrt_fusion.2), kind=kOutput, calls=%fused_computation.2 | convolution fusion | flops 1880965120 | bytes 33816832 | tf_op jit(solution)/shard_map/dot_general | solution.py:27
  294.2 0.3 all-gather.23.cloned.1.call-start
  294.5 131.7 %all-gather.21.cloned.1.call-done = f32[1024,8192]{1,0:T(8,128)} async-done(((f32[64,8192]{1,0:T(8,128)}), f32[1024,8192]{1,0:T(8,128)}) %all-gather.21.cloned.1.call-update) | async-done | bytes 33554448 | tf_op jit(solution)/shard_map/all_gather | solution.py:28
  426.1 12.7 %reduce_sum.77 = f32[64,8192]{1,0:T(8,128)S(1)} reduce(f32[16,64,8192]{2,1,0:T(8,128)} %bitcast.83, f32[]{:T(128)} %constant.18.clone.1), dimensions={0}, to_apply=%region_5.6 | reduce | flops 7864320 | bytes 35651588 | tf_op jit(solution)/shard_map/reduce_sum | solution.py:28
  438.8 0.4 multiply_reduce_fusion
  439.2 1.3 copy-done.3
  440.6 6.9 fusion.8
  447.5 15.1 %fusion = f32[64,8192]{1,0:T(8,128)} fusion(bf16[2,896,8192]{2,1,0:T(8,128)(2,1)} %param.9, bf16[2,8192,896]{2,1,0:T(8,128)(2,1)} %param.8, f32[64,896]{1,0:T(8,128)S(1)} %fusion.8, f32[64,8192]{1,0:T(8,128)} %copy-done.3, f32[64]{0:T(128)S(1)} %add_rsqrt_fusion, f32[8192]{0:T(1024)S(1)} %bitcast.89), kind=kOutput, calls=%fused_computation | convolution fusion | flops 1880965120 | bytes 33816832 | tf_op jit(solution)/shard_map/dot_general | solution.py:27
  462.7 132.9 %all-gather.17.cloned.1.call-done = f32[1024,8192]{1,0:T(8,128)} async-done(((f32[64,8192]{1,0:T(8,128)}), f32[1024,8192]{1,0:T(8,128)}) %all-gather.17.cloned.1.call-update) | async-done | bytes 33554448 | tf_op jit(solution)/shard_map/all_gather | solution.py:28
  595.6 12.7 %reduce_sum.75 = f32[64,8192]{1,0:T(8,128)S(1)} reduce(f32[16,64,8192]{2,1,0:T(8,128)} %bitcast.82, f32[]{:T(128)} %constant.18.clone.1), dimensions={0}, to_apply=%region_3.4 | reduce | flops 7864320 | bytes 35651588 | tf_op jit(solution)/shard_map/reduce_sum | solution.py:28
  608.3 156.8 %all-gather.23.cloned.1.call-done = f32[1024,8192]{1,0:T(8,128)} async-done(((f32[64,8192]{1,0:T(8,128)}), f32[1024,8192]{1,0:T(8,128)}) %all-gather.23.cloned.1.call-update) | async-done | bytes 33554448 | tf_op jit(solution)/shard_map/all_gather | solution.py:28
  765.1 13.0 %reduce_sum.79 = f32[64,8192]{1,0:T(8,128)} reduce(f32[16,64,8192]{2,1,0:T(8,128)} %bitcast.85, f32[]{:T(128)} %constant.18.clone.1), dimensions={0}, to_apply=%region_7.8 | reduce | flops 7864320 | bytes 35651588 | tf_op jit(solution)/shard_map/reduce_sum | solution.py:28
  778.1 0.9 fusion.110
  779.1 1.0 fusion.111
  780.1 0.7 pad_maximum_fusion
  (19 shorter events, 0.2 us)
Async XLA Ops:
  6.5 42.4 %all-gather.13.cloned.1.call-start = ((), (), s32[]{:S(2)}) async-start(), calls=%async_computation | async-start | bytes 1114112 | tf_op jit(solution)/shard_map/all_gather | solution.py:14
  8.1 79.2 %all-gather.19.cloned.1.call-start = ((), (), s32[]{:S(2)}) async-start(), calls=%async_computation.3 | async-start | bytes 1114112 | tf_op jit(solution)/shard_map/all_gather | solution.py:14
  8.8 247.8 %all-gather.15.cloned.1.call-start = ((), (), s32[]{:S(2)}) async-start(), calls=%async_computation.1 | async-start | bytes 35651584 | tf_op jit(solution)/shard_map/all_gather | solution.py:28
  50.4 8.2 %copy-start.1 = (bf16[1,64,8192]{2,1,0:T(8,128)(2,1)S(1)}, bf16[1,64,8192]{2,1,0:T(8,128)(2,1)}, u32[]{:S(2)}) copy-start(bf16[1,64,8192]{2,1,0:T(8,128)(2,1)} %all-gather.13.cloned.1.call-done) | copy-start | bytes 3145732
  75.0 351.1 %all-gather.21.cloned.1.call-start = ((), (), s32[]{:S(2)}) async-start(), calls=%async_computation.4 | async-start | bytes 35651584 | tf_op jit(solution)/shard_map/all_gather | solution.py:28
  88.9 8.2 %copy-start = (bf16[1,64,8192]{2,1,0:T(8,128)(2,1)S(1)}, bf16[1,64,8192]{2,1,0:T(8,128)(2,1)}, u32[]{:S(2)}) copy-start(bf16[1,64,8192]{2,1,0:T(8,128)(2,1)} %all-gather.19.cloned.1.call-done) | copy-start | bytes 3145732
  113.8 481.8 %all-gather.17.cloned.1.call-start = ((), (), s32[]{:S(2)}) async-start(), calls=%async_computation.2 | async-start | bytes 35651584 | tf_op jit(solution)/shard_map/all_gather | solution.py:28
  270.9 1.3 copy-start.2
  294.2 470.9 %all-gather.23.cloned.1.call-start = ((), (), s32[]{:S(2)}) async-start(), calls=%async_computation.5 | async-start | bytes 35651584 | tf_op jit(solution)/shard_map/all_gather | solution.py:28
  439.2 1.4 copy-start.3
Sparse Core Ops, SparseCore 0:
  9.5 39.3 all-gather.12
  51.0 36.2 all-gather.18
  88.9 167.6 all-gather.14
  258.1 168.0 all-gather.20
  427.6 168.0 all-gather.16
  597.1 168.0 all-gather.22
